TPU v7x, 128 devices: a whole 4x4x4 slice. The times are simulated.
128 devices in a mesh: pb: 16 (over y, x_hi, core), ka: 8 (over z, x_lo).
Axes of the slice: x: 4 (x_hi: 2, x_lo: 2; x = x_hi * 2 + x_lo), y: 4, z: 4, core: 2. Of those that a mesh axis runs over, the one named last changes fastest.
Arguments:
- bin_states: bfloat16 [8192, 1536], P(('pb', 'ka')), may hold values from -50 to 50
- contacts: int32 [8192, 16384], P('pb', 'ka'), may hold values from 0 to 2047, as said below
- w_query: bfloat16 [1536, 256], replicated, may hold values from -0.15625 to 0.15625
- w_keyval: bfloat16 [1536, 512], replicated, may hold values from -0.15625 to 0.15625
- pair_in: float32 [2, 32], replicated, may hold values from -30 to 30
- pair_shift: float32 [2, 32], replicated, may hold values from -230 to 230
- pair_out: float32 [2, 32], replicated, may hold values from -2.7 to 2.7
- w_out: bfloat16 [256, 1536], replicated, may hold values from -0.375 to 0.375
Outputs:
- mixed_out: bfloat16 [8192, 1536], P(('pb', 'ka'))
Inputs may be any that keep to these rules, and one draw needn't show every extreme that they name: contacts fall off with the distance |c - 8192|; the count at offset zero reaches 2047 in every draw.
All inputs are finite; a program needn't handle non-finite values.
Results may differ from a plain program's by a relative error of at most 0.012.
The roundings to bfloat16 on the way count: a program that leaves them out, or rounds other values in their place, can miss the bound.
Values may be sent and summed in bfloat16 or wider, within the bound.
A program may use at most 128 MiB of HBM per device.

v0:
```python
import jax
import jax.numpy as jnp
from jax import lax
from jax.sharding import PartitionSpec as P

HEADS = 2
HEAD_DIM = 128
PAIR_HIDDEN = 32
HALF_BAND = 8192


def shifted(block, axis, distance):
    devices = range(lax.axis_size(axis))
    route = [((i - distance) % len(devices), i) for i in devices]
    return lax.ppermute(block, axis, route)


def shear_rows(tile):
    leading, height, length = tile.shape
    padded = jnp.pad(tile, ((0, 0), (0, 0), (0, height + 1)))
    flattened = padded.reshape(leading, height * (length + height + 1))
    flattened = flattened[:, : height * (length + height)]
    return flattened.reshape(leading, height, length + height)


def pair_bias(pair_counts, pair_in, pair_shift, pair_out):
    log_counts = jnp.log(1.0 + pair_counts.astype(jnp.float32))
    per_head = []
    for head_index in range(HEADS):
        summed = jnp.zeros(log_counts.shape, jnp.float32)
        for hidden_unit in range(PAIR_HIDDEN):
            inner = (
                pair_in[head_index, hidden_unit] * log_counts + pair_shift[head_index, hidden_unit]
            )
            summed = summed + pair_out[head_index, hidden_unit] * jax.nn.silu(inner)
        per_head.append(summed)
    return jnp.stack(per_head, 0)


def shards(bin_states, contacts, w_query, w_keyval, pair_in, pair_shift, pair_out, w_out):
    head_cols = HEADS * HEAD_DIM
    queries = jnp.dot(bin_states, w_query, preferred_element_type=jnp.float32).astype(jnp.bfloat16)
    key_values = jnp.dot(bin_states, w_keyval, preferred_element_type=jnp.float32).astype(
        jnp.bfloat16
    )
    query_block, keyval_block = (
        lax.all_gather(queries, "ka", axis=0, tiled=True),
        lax.all_gather(key_values, "ka", axis=0, tiled=True),
    )
    pb_count = lax.axis_size("pb")
    ka_count = lax.axis_size("ka")
    pb_index = lax.axis_index("pb")
    ka_index = lax.axis_index("ka")
    query_rows = query_block.shape[0]
    offsets = contacts.shape[1]
    span_ratio = offsets // query_rows
    lead_blocks = HALF_BAND // query_rows
    seq_len = query_rows * pb_count
    key_start = pb_index * query_rows + ka_index * offsets - HALF_BAND
    pieces = []
    for step_index in range(span_ratio + 1):
        amount = (lead_blocks - step_index) % pb_count
        if amount == 0:
            pieces.append(keyval_block)
        else:
            pieces.append(shifted(keyval_block, "pb", amount))
    key_window = jnp.concatenate(pieces, 0)
    for bit_pos in range(ka_count.bit_length() - 1):
        amount = -(span_ratio << bit_pos) % pb_count
        if amount != 0:
            arrived = shifted(key_window, "pb", amount)
            key_window = jnp.where(ka_index >> bit_pos & 1 == 1, arrived, key_window)
    sub_rows = min(512, query_rows)
    sub_count = query_rows // sub_rows
    key_span = sub_rows + offsets
    inv_root = 1.0 / HEAD_DIM**0.5
    row_pos = jnp.arange(sub_rows, dtype=jnp.int32)[:, None]
    col_pos = jnp.arange(key_span, dtype=jnp.int32)[None, :]

    def score_block(block_index):
        first_row = block_index * sub_rows
        rows_query = query_block.reshape(sub_rows, HEADS, HEAD_DIM)
        keys_here = key_window[:, :head_cols]
        key_heads = keys_here.reshape(key_span, HEADS, HEAD_DIM)
        bias_tile = shear_rows(pair_bias(contacts, pair_in, pair_shift, pair_out))
        scores = (
            jnp.einsum("ihd,khd->hik", rows_query, key_heads, preferred_element_type=jnp.float32)
            * inv_root
            + bias_tile
        )
        key_pos = key_start + first_row + col_pos
        allowed = (
            (col_pos >= row_pos)
            & (col_pos < row_pos + offsets)
            & (key_pos >= 0)
            & (key_pos < seq_len)
        )
        return jnp.where(allowed[None], scores, -1e30)

    block_ids = jnp.arange(sub_count, dtype=jnp.int32)
    scores = lax.map(score_block, block_ids)
    row_top = lax.pmax(jnp.max(scores, axis=3), "ka")

    def weigh_block(operands):
        block_scores, block_top, block_index = operands
        weights = jnp.exp(block_scores - block_top[:, :, None]).astype(jnp.bfloat16)
        totals = jnp.sum(weights, axis=2, dtype=jnp.float32)
        values_here = key_window[:, head_cols:]
        value_heads = values_here.reshape(key_span, HEADS, HEAD_DIM)
        numerators = jnp.einsum(
            "hik,khd->ihd", weights, value_heads, preferred_element_type=jnp.float32
        )
        return (numerators.reshape(sub_rows, head_cols), jnp.transpose(totals))

    numerators, totals = lax.map(weigh_block, (scores, row_top, block_ids))
    numerators = numerators.reshape(query_rows, head_cols)
    totals = totals.reshape(query_rows, HEADS)
    share_rows = query_rows // ka_count
    summed_num, summed_tot = lax.psum((numerators, totals), "ka")
    first_share = ka_index * share_rows
    summed_num = lax.dynamic_slice_in_dim(summed_num, first_share, share_rows, 0)
    summed_tot = lax.dynamic_slice_in_dim(summed_tot, first_share, share_rows, 0)
    attended = summed_num.reshape(share_rows, HEADS, HEAD_DIM) / summed_tot[:, :, None]
    attended = attended.reshape(share_rows, head_cols).astype(jnp.bfloat16)
    return jnp.dot(attended, w_out, preferred_element_type=jnp.float32).astype(jnp.bfloat16)


def solution(mesh):
    placed = (P(("pb", "ka"), None), P("pb", "ka"), P(), P(), P(), P(), P(), P())
    return jax.shard_map(
        shards, mesh=mesh, in_specs=placed, out_specs=P(("pb", "ka"), None), check_vma=False
    )
```

profile of v0, /device:TPU:0, one launch (start us, length us, event | category | flops | bytes accessed | tf_op | source)
XLA Modules:
  0.0 525.7 jit_solution(3791947021305828865)
XLA Ops:
  6.5 0.0 copy-start
  6.5 0.0 all-reduce.3.cloned.1.call-start
  6.5 1.4 copy-done
  7.9 1.5 convolution_convert_fusion.1
  9.4 31.4 %all_gather.6 = bf16[512,512]{1,0:T(8,128)(2,1)S(1)} all-gather(bf16[64,512]{1,0:T(8,128)(2,1)S(1)} %convolution_convert_fusion.1), channel_id=1, replica_groups=mesh['pb'=16,'ka'=8] {'ka'}, dimensions={0}, use_global_device_ids=true | all-gather | bytes 589824 | tf_op jit(solution)/shard_map/all_gather | solution.py:48
  40.8 0.0 collective-permute-start
  40.9 5.4 %collective-permute-start.1 = (bf16[512,512]{1,0:T(8,128)(2,1)S(1)}, bf16[512,512]{1,0:T(8,128)(2,1)S(1)}, u32[]{:S(2)}, u32[]{:S(2)}) collective-permute-start(bf16[512,512]{1,0:T(8,128)(2,1)S(1)} %all_gather.6), channel_id=1, source_target_pairs={{16,0},{24,8},{32,16},{40,24},{48,32},{56,40},{64,48},{72,56},{80,... | collective-permute-start | bytes 1572872 | tf_op jit(solution)/shard_map/ppermute | solution.py:15
  46.2 0.6 collective-permute-start.2
  46.8 0.4 collective-permute-start.3
  47.3 2.1 fusion.14
  49.4 2.1 fusion.17
  51.5 2.1 fusion.13
  53.5 2.1 fusion.16
  55.6 2.1 fusion.12
  57.7 2.1 fusion.15
  59.8 1.6 fusion.23
  61.5 1.6 fusion.22
  63.1 1.6 fusion.21
  64.7 0.8 constant_dynamic-update-slice_fusion.4
  65.5 0.0 collective-permute-done
  65.5 0.8 constant_dynamic-update-slice_fusion.3
  66.4 1.3 collective-permute-done.1
  67.6 0.8 constant_dynamic-update-slice_fusion.2
  68.5 0.0 collective-permute-done.2
  68.5 0.8 constant_dynamic-update-slice_fusion.1
  69.3 0.0 collective-permute-done.3
  69.3 0.8 constant_dynamic-update-slice_fusion
  70.2 3.0 collective-permute-start.4
  73.2 0.0 copy-done.9
  73.2 113.2 %add_bitcast_fusion = f32[1,512,2048]{2,1,0:T(8,128)} fusion(s32[512,2048]{1,0:T(8,128)S(1)} %copy-done.9, f32[]{:T(128)} %bitcast.193, f32[]{:T(128)} %bitcast.192, f32[]{:T(128)} %bitcast.191, f32[]{:T(128)} %bitcast.190, f32[]{:T(128)} %bitcast.189, f32[]{:T(128)} %bitcast.188, f32[]{:T(128)} %bitcast.187, f32[]{:T(128)} %bitcast.186, f32[]{:T(128)} %bitcast.185, ...), kind=kLoop, calls=%fused_computation.11 | loop fusion | flops 269484032 | bytes 8388992 | tf_op jit(solution)/shard_map/while/body/eval_jaxpr/stack | solution.py:37
  186.3 0.0 copy-done.3
  186.3 0.7 fusion.20
  187.1 0.0 copy-done.4
  187.1 0.7 fusion.19
  187.8 0.0 copy-done.5
  187.8 0.7 fusion.18
  188.5 0.0 collective-permute-done.4
  188.5 3.6 broadcast_select_fusion
  192.1 0.6 collective-permute-start.5
  192.7 0.0 copy-done.10
  192.7 112.8 %add_bitcast_fusion.1 = f32[1,512,2048]{2,1,0:T(8,128)} fusion(s32[512,2048]{1,0:T(8,128)S(1)} %copy-done.10, f32[]{:T(128)} %bitcast.96, f32[]{:T(128)} %bitcast.95, f32[]{:T(128)} %bitcast.94, f32[]{:T(128)} %bitcast.93, f32[]{:T(128)} %bitcast.92, f32[]{:T(128)} %bitcast.91, f32[]{:T(128)} %bitcast.90, f32[]{:T(128)} %bitcast.89, f32[]{:T(128)} %bitcast.88, ...), kind=kLoop, calls=%fused_computation.12 | loop fusion | flops 269484032 | bytes 8388992 | tf_op jit(solution)/shard_map/while/body/eval_jaxpr/stack | solution.py:37
  305.5 8.5 %select_maximum_fusion = f32[2,512,2561]{2,1,0:T(8,128)} fusion(f32[1,512,2048]{2,1,0:T(8,128)} %add_bitcast_fusion, f32[1,512,2048]{2,1,0:T(8,128)} %add_bitcast_fusion.1), kind=kLoop, calls=%fused_computation | loop fusion | flops 10489856 | bytes 18878464 | tf_op jit(solution)/shard_map/while/body/eval_jaxpr/stack | solution.py:37
  314.1 15.9 %reshape.122 = f32[2622464]{0:T(1024)} reshape(f32[2,512,2561]{2,1,0:T(8,128)} %select_maximum_fusion) | data formatting | bytes 20979712
  330.0 16.6 %reshape.118 = f32[2,1311232]{1,0:T(2,128)} reshape(f32[2622464]{0:T(1024)} %reshape.122) | data formatting | bytes 20979712 | tf_op jit(solution)/shard_map/while/body/eval_jaxpr/reshape | solution.py:21
  346.6 8.5 %slice.977 = f32[2,1310720]{1,0:T(2,128)} slice(f32[2,1311232]{1,0:T(2,128)} %reshape.118), slice={[0:2], [0:1310720]} | slice | bytes 20971520 | tf_op jit(solution)/shard_map/while/body/eval_jaxpr/slice | solution.py:22
  355.2 0.3 convolution_convert_fusion.2
  355.4 29.0 %all_gather.7 = bf16[512,256]{1,0:T(8,128)(2,1)S(1)} all-gather(bf16[64,256]{1,0:T(8,128)(2,1)S(1)} %convolution_convert_fusion.2), channel_id=1, replica_groups=mesh['pb'=16,'ka'=8] {'ka'}, dimensions={0}, use_global_device_ids=true | all-gather | bytes 294912 | tf_op jit(solution)/shard_map/all_gather | solution.py:47
  384.4 1.3 fusion.3
  385.7 0.0 collective-permute-done.5
  385.7 2.0 broadcast_select_fusion.1
  387.8 1.4 slice_bitcast_fusion
  389.1 1.6 copy.15
  390.7 10.8 %fusion.24 = (f32[2,512]{1,0:T(2,128)S(1)}, f32[2,512,2560]{2,1,0:T(8,128)}) fusion(f32[1,2,512,2560]{3,1,2,0:T(2,128)} %bitcast.233, bf16[320,2,8,128]{3,2,1,0:T(8,128)(2,1)} %get-tuple-element.31, pred[512,2560]{1,0:T(8,128)(4,1)S(1)} %fusion.3, bf16[512,256]{1,0:T(8,128)(2,1)S(1)} %all_gather.7), kind=kOutput, calls=%fused_computation.49 | convolution fusion | flops 681573376 | bytes 23859200 | tf_op jit(solution)/shard_map/while/body/eval_jaxpr/ihd,khd->hik/dot_general | solution.py:87
  401.5 18.0 %pmax.7 = f32[2,512]{1,0:T(2,128)S(1)} all-reduce(f32[2,512]{1,0:T(2,128)S(1)} %get-tuple-element.250), channel_id=1, replica_groups=mesh['pb'=16,'ka'=8] {'ka'}, use_global_device_ids=true, to_apply=%region_1.2 | all-reduce | flops 1024 | bytes 8192 | tf_op jit(solution)/shard_map/pmax | solution.py:102
  419.5 6.7 %fusion.4 = f32[2,128,512]{2,1,0:T(8,128)} fusion(bf16[2560,2,128]{0,2,1:T(8,128)(2,1)S(1)} %bitcast.234, f32[2,512,2560]{2,1,0:T(8,128)} %get-tuple-element.251, f32[2,512]{1,0:T(2,128)S(1)} %pmax.7), kind=kOutput, calls=%fused_computation.17 | convolution fusion | flops 676331520 | bytes 12324864 | tf_op jit(solution)/shard_map/while/body/eval_jaxpr/hik,khd->ihd/dot_general | solution.py:110
  426.2 0.0 all-reduce.3.cloned.1.call-update
  426.3 0.0 copy-start.6
  426.3 0.0 copy-start.1
  426.3 5.6 %convert_reduce_fusion = f32[2,512]{1,0:T(2,128)S(1)} fusion(f32[2,512,2560]{2,1,0:T(8,128)} %get-tuple-element.251, f32[2,512]{1,0:T(2,128)S(1)} %pmax.7), kind=kLoop, calls=%fused_computation.4 | loop fusion | flops 10484736 | bytes 10493952 | tf_op jit(solution)/shard_map/while/body/eval_jaxpr/reduce_sum | solution.py:107
  431.9 16.1 %psum.15 = f32[512,2]{0,1:T(2,128)S(1)} all-reduce(f32[512,2]{0,1:T(2,128)S(1)} %bitcast.236), channel_id=1, replica_groups=mesh['pb'=16,'ka'=8] {'ka'}, use_global_device_ids=true, to_apply=%region_4.5 | all-reduce | flops 1024 | bytes 8192 | tf_op jit(solution)/shard_map/psum | solution.py:119
  448.0 0.1 constant_dynamic-slice_fusion
  448.1 68.8 %all-reduce.3.cloned.1.call-done = f32[512,256]{0,1:T(8,128)} async-done(((f32[512,256]{0,1:T(8,128)}), f32[512,256]{0,1:T(8,128)}) %all-reduce.3.cloned.1.call-update) | async-done | bytes 524304 | tf_op jit(solution)/shard_map/psum | solution.py:119
  516.9 1.0 fusion.9
  517.9 1.0 convolution_convert_fusion
  (15 shorter events, 0.0 us)
Async XLA Ops:
  6.5 1.4 copy-start
  6.5 510.3 %all-reduce.3.cloned.1.call-start = ((), (), s32[]{:S(2)}) async-start(), calls=%async_computation | async-start | bytes 1048576 | tf_op jit(solution)/shard_map/psum | solution.py:119
  7.9 65.2 %copy-start.9 = (s32[512,2048]{1,0:T(8,128)S(1)}, s32[512,2048]{1,0:T(8,128)}, u32[]{:S(2)}) copy-start(s32[512,2048]{1,0:T(8,128)} %param.9) | copy-start | bytes 12582916
  40.8 24.7 %collective-permute-start = (bf16[512,512]{1,0:T(8,128)(2,1)S(1)}, bf16[512,512]{1,0:T(8,128)(2,1)S(1)}, u32[]{:S(2)}, u32[]{:S(2)}) collective-permute-start(bf16[512,512]{1,0:T(8,128)(2,1)S(1)} %all_gather.6), channel_id=1, source_target_pairs={{8,0},{16,8},{24,16},{32,24},{40,32},{48,40},{56,48},{64,56},{72,6... | collective-permute-start | bytes 1572872 | tf_op jit(solution)/shard_map/ppermute | solution.py:15
  40.9 26.8 %collective-permute-start.1 = (bf16[512,512]{1,0:T(8,128)(2,1)S(1)}, bf16[512,512]{1,0:T(8,128)(2,1)S(1)}, u32[]{:S(2)}, u32[]{:S(2)}) collective-permute-start(bf16[512,512]{1,0:T(8,128)(2,1)S(1)} %all_gather.6), channel_id=1, source_target_pairs={{16,0},{24,8},{32,16},{40,24},{48,32},{56,40},{64,48},{72,56},{80,... | collective-permute-start | bytes 1572872 | tf_op jit(solution)/shard_map/ppermute | solution.py:15
  46.2 22.3 %collective-permute-start.2 = (bf16[512,512]{1,0:T(8,128)(2,1)S(1)}, bf16[512,512]{1,0:T(8,128)(2,1)S(1)}, u32[]{:S(2)}, u32[]{:S(2)}) collective-permute-start(bf16[512,512]{1,0:T(8,128)(2,1)S(1)} %all_gather.6), channel_id=1, source_target_pairs={{24,0},{32,8},{40,16},{48,24},{56,32},{64,40},{72,48},{80,56},{88,... | collective-permute-start | bytes 1572872 | tf_op jit(solution)/shard_map/ppermute | solution.py:15
  46.8 22.5 %collective-permute-start.3 = (bf16[512,512]{1,0:T(8,128)(2,1)S(1)}, bf16[512,512]{1,0:T(8,128)(2,1)S(1)}, u32[]{:S(2)}, u32[]{:S(2)}) collective-permute-start(bf16[512,512]{1,0:T(8,128)(2,1)S(1)} %all_gather.6), channel_id=1, source_target_pairs={{32,0},{40,8},{48,16},{56,24},{64,32},{72,40},{80,48},{88,56},{96,... | collective-permute-start | bytes 1572872 | tf_op jit(solution)/shard_map/ppermute | solution.py:15
  70.2 118.4 %collective-permute-start.4 = (bf16[2560,512]{1,0:T(8,128)(2,1)}, bf16[2560,512]{1,0:T(8,128)(2,1)}, u32[]{:S(2)}, u32[]{:S(2)}) collective-permute-start(bf16[2560,512]{1,0:T(8,128)(2,1)} %constant_dynamic-update-slice_fusion), channel_id=1, source_target_pairs={{32,0},{40,8},{48,16},{56,24},{64,32},{72,40},{80,48},{88,56},{96,... | collective-permute-start | bytes 7864328 | tf_op jit(solution)/shard_map/ppermute | solution.py:15
  73.2 113.2 %copy-start.3 = (f32[2,32]{1,0:T(2,128)S(1)}, f32[2,32]{1,0:T(2,128)}, u32[]{:S(2)}) copy-start(f32[2,32]{1,0:T(2,128)} %param.13) | copy-start | bytes 772
  73.2 113.9 %copy-start.4 = (f32[2,32]{1,0:T(2,128)S(1)}, f32[2,32]{1,0:T(2,128)}, u32[]{:S(2)}) copy-start(f32[2,32]{1,0:T(2,128)} %param.12) | copy-start | bytes 772
  73.2 114.6 %copy-start.5 = (f32[2,32]{1,0:T(2,128)S(1)}, f32[2,32]{1,0:T(2,128)}, u32[]{:S(2)}) copy-start(f32[2,32]{1,0:T(2,128)} %param.14) | copy-start | bytes 772
  186.3 6.4 %copy-start.10 = (s32[512,2048]{1,0:T(8,128)S(1)}, s32[512,2048]{1,0:T(8,128)}, u32[]{:S(2)}) copy-start(s32[512,2048]{1,0:T(8,128)} %param.9) | copy-start | bytes 12582916
  192.1 193.6 %collective-permute-start.5 = (bf16[2560,512]{1,0:T(8,128)(2,1)}, bf16[2560,512]{1,0:T(8,128)(2,1)}, u32[]{:S(2)}, u32[]{:S(2)}) collective-permute-start(bf16[2560,512]{1,0:T(8,128)(2,1)} %broadcast_select_fusion), channel_id=1, source_target_pairs={{64,0},{72,8},{80,16},{88,24},{96,32},{104,40},{112,48},{120,56},{... | collective-permute-start | bytes 7864328 | tf_op jit(solution)/shard_map/ppermute | solution.py:15
  346.6 8.6 %copy-start.7 = (bf16[1536,256]{1,0:T(8,128)(2,1)S(1)}, bf16[1536,256]{1,0:T(8,128)(2,1)}, u32[]{:S(2)}) copy-start(bf16[1536,256]{1,0:T(8,128)(2,1)} %param.10) | copy-start | bytes 2359300
  346.6 8.6 %copy-start.8 = (bf16[64,1536]{1,0:T(8,128)(2,1)S(1)}, bf16[64,1536]{1,0:T(8,128)(2,1)}, u32[]{:S(2)}) copy-start(bf16[64,1536]{1,0:T(8,128)(2,1)} %param.8) | copy-start | bytes 589828
  390.7 28.8 %copy-start.2 = (bf16[2560,256]{0,1:T(8,128)(2,1)S(1)}, bf16[2560,256]{0,1:T(8,128)(2,1)}, u32[]{:S(2)}) copy-start(bf16[2560,256]{0,1:T(8,128)(2,1)} %copy.15) | copy-start | bytes 3932164
  426.3 91.6 %copy-start.6 = (bf16[256,1536]{1,0:T(8,128)(2,1)S(1)}, bf16[256,1536]{1,0:T(8,128)(2,1)}, u32[]{:S(2)}) copy-start(bf16[256,1536]{1,0:T(8,128)(2,1)} %param.15) | copy-start | bytes 2359300
  426.3 92.6 %copy-start.1 = (bf16[1536,512]{1,0:T(8,128)(2,1)S(1)}, bf16[1536,512]{1,0:T(8,128)(2,1)}, u32[]{:S(2)}) copy-start(bf16[1536,512]{1,0:T(8,128)(2,1)} %param.11) | copy-start | bytes 4718596
Sparse Core Ops, SparseCore 0:
  426.4 90.4 all-reduce.2
where the time goes:
time: 528 us; the launch traced here: 526 us
  other arithmetic  248 us (47%)
  blocking collectives  94.5 us (18%)
  waiting for transfers between devices  70.1 us (13%)
  local copies, waits for them, and re-layouts  69.3 us (13%)
  matrix products  20.2 us (4%)
  between operations  13.5 us (3%)
  starting transfers between devices  10 us (2%)
    another operation x3, other arithmetic, pair_bias(): return jnp.stack(per_head, 0)  234 us
    psum x1, waiting for transfers between devices, shards(): summed_num, summed_tot = lax.psum((numerators, totals), 'ka')  68.8 us
    all_gather x1, blocking collectives, shards(): lax.all_gather(key_values, 'ka', axis=0, tiled=True)  31.4 us
    all_gather x1, blocking collectives, shards(): lax.all_gather(queries, 'ka', axis=0, tiled=True)  29 us
    unnamed x28, local copies, waits for them, and re-layouts  22.1 us
    pmax x1, blocking collectives, shards(): row_top = lax.pmax(jnp.max(scores, axis=3), 'ka')  18 us
    reshape x1, local copies, waits for them, and re-layouts, shear_rows(): flattened = padded.reshape(leading, height * (length + height + 1))  16.6 us
    psum x1, blocking collectives, shards(): summed_num, summed_tot = lax.psum((numerators, totals), 'ka')  16.1 us
  transfers between devices with their start and end apart: 7, of which 2 were waited for; matrix products, arithmetic and copies ran while one was open for 58% of the time, Pallas kernels for 0%

commit v1 on v0

--- a/solution.py
+++ b/solution.py
@@ -44,7 +44,9 @@
         jnp.bfloat16
     )
     query_block, keyval_block = (
-        lax.all_gather(queries, "ka", axis=0, tiled=True),
+        jnp.concatenate(
+            lax.all_to_all(jnp.stack([queries] * lax.axis_size("ka")), "ka", 0, 0), axis=0
+        ),
         lax.all_gather(key_values, "ka", axis=0, tiled=True),
     )
     pb_count = lax.axis_size("pb")

time: 528 us -> 499 us (0.945)
  blocking collectives: 94.5 us -> 66.5 us
  local copies, waits for them, and re-layouts: 69.3 us -> 59 us
    all_gather x1 -> x0, blocking collectives: 29 us -> none  [shards(): lax.all_gather(queries, 'ka', axis=0, tiled=True)]
    unnamed x28 -> x24, local copies, waits for them, and re-layouts: 22.1 us -> 22.1 us
  transfers between devices with their start and end apart: 7 -> 8, of which waited for: 2 -> 2; matrix products, arithmetic and copies ran while one was open for 58% -> 61% of each run, Pallas kernels for 0% -> 0%
where the time goes in v1:
time: 499 us; the launch traced here: 497 us
  other arithmetic  248 us (50%)
  waiting for transfers between devices  73.9 us (15%)
  blocking collectives  66.5 us (13%)
  local copies, waits for them, and re-layouts  59 us (12%)
  matrix products  21.3 us (4%)
  starting transfers between devices  14.2 us (3%)
  between operations  13.5 us (3%)
    another operation x3, other arithmetic, pair_bias(): return jnp.stack(per_head, 0)  234 us
    psum x1, waiting for transfers between devices, shards(): summed_num, summed_tot = lax.psum((numerators, totals), 'ka')  68 us
    all_gather x1, blocking collectives, shards(): lax.all_gather(key_values, 'ka', axis=0, tiled=True)  31.4 us
    unnamed x24, local copies, waits for them, and re-layouts  22.1 us
    pmax x1, blocking collectives, shards(): row_top = lax.pmax(jnp.max(scores, axis=3), 'ka')  19.1 us
    reshape x1, local copies, waits for them, and re-layouts, shear_rows(): flattened = padded.reshape(leading, height * (length + height + 1))  16.6 us
    psum x1, blocking collectives, shards(): summed_num, summed_tot = lax.psum((numerators, totals), 'ka')  16 us
    dot_general x1, matrix products, score_block(): jnp.einsum('ihd,khd->hik', rows_query, key_heads, preferred_element_type=...  10.8 us
  transfers between devices with their start and end apart: 8, of which 2 were waited for; matrix products, arithmetic and copies ran while one was open for 61% of the time, Pallas kernels for 0%

profile of v1, /device:TPU:0, one launch (start us, length us, event | category | flops | bytes accessed | tf_op | source)
XLA Modules:
  0.0 496.5 jit_solution(14549392485045058470)
XLA Ops:
  6.5 0.0 copy-start
  6.5 1.4 copy-done
  7.9 1.3 convolution_convert_fusion.1
  9.3 31.4 %all_gather.3 = bf16[512,512]{1,0:T(8,128)(2,1)S(1)} all-gather(bf16[64,512]{1,0:T(8,128)(2,1)S(1)} %convolution_convert_fusion.1), channel_id=1, replica_groups=mesh['pb'=16,'ka'=8] {'ka'}, dimensions={0}, use_global_device_ids=true | all-gather | bytes 589824 | tf_op jit(solution)/shard_map/all_gather | solution.py:50
  40.7 0.0 collective-permute-start
  40.7 5.4 %collective-permute-start.1 = (bf16[512,512]{1,0:T(8,128)(2,1)S(1)}, bf16[512,512]{1,0:T(8,128)(2,1)S(1)}, u32[]{:S(2)}, u32[]{:S(2)}) collective-permute-start(bf16[512,512]{1,0:T(8,128)(2,1)S(1)} %all_gather.3), channel_id=1, source_target_pairs={{16,0},{24,8},{32,16},{40,24},{48,32},{56,40},{64,48},{72,56},{80,... | collective-permute-start | bytes 1572872 | tf_op jit(solution)/shard_map/ppermute | solution.py:15
  46.1 0.6 collective-permute-start.2
  46.7 0.4 collective-permute-start.3
  47.1 1.5 convolution_convert_fusion.2
  48.6 0.7 stack.11
  49.3 4.1 all-to-all-start
  53.4 0.0 all-reduce.3.cloned.1.call-start
  53.5 0.0 copy-start.7
  53.5 0.7 fusion.13
  54.2 0.7 fusion.16
  55.0 0.7 fusion.12
  55.7 0.7 fusion.15
  56.4 0.7 fusion.11
  57.2 0.7 fusion.14
  57.9 0.7 fusion.22
  58.6 0.7 fusion.21
  59.3 0.7 fusion.20
  59.9 0.8 constant_dynamic-update-slice_fusion.4
  60.8 0.0 collective-permute-done
  60.8 0.8 constant_dynamic-update-slice_fusion.3
  61.6 5.9 %collective-permute-done.1 = bf16[512,512]{1,0:T(8,128)(2,1)S(1)} collective-permute-done((bf16[512,512]{1,0:T(8,128)(2,1)S(1)}, bf16[512,512]{1,0:T(8,128)(2,1)S(1)}, u32[]{:S(2)}, u32[]{:S(2)}) %collective-permute-start.1) | collective-permute-done | bytes 524320 | tf_op jit(solution)/shard_map/ppermute | solution.py:15
  67.5 0.8 constant_dynamic-update-slice_fusion.2
  68.3 0.0 collective-permute-done.2
  68.3 0.8 constant_dynamic-update-slice_fusion.1
  69.2 0.0 collective-permute-done.3
  69.2 0.8 constant_dynamic-update-slice_fusion
  70.0 3.0 collective-permute-start.4
  73.0 113.1 %add_bitcast_fusion = f32[1,512,2048]{2,1,0:T(8,128)} fusion(s32[512,2048]{1,0:T(8,128)S(1)} %copy-done.7, f32[]{:T(128)} %bitcast.193, f32[]{:T(128)} %bitcast.192, f32[]{:T(128)} %bitcast.191, f32[]{:T(128)} %bitcast.190, f32[]{:T(128)} %bitcast.189, f32[]{:T(128)} %bitcast.188, f32[]{:T(128)} %bitcast.187, f32[]{:T(128)} %bitcast.186, f32[]{:T(128)} %bitcast.185, ...), kind=kLoop, calls=%fused_computation.11 | loop fusion | flops 269484032 | bytes 8388992 | tf_op jit(solution)/shard_map/while/body/eval_jaxpr/stack | solution.py:37
  186.1 0.7 fusion.19
  186.9 0.7 fusion.18
  187.6 0.7 fusion.17
  188.3 0.0 collective-permute-done.4
  188.3 3.6 broadcast_select_fusion
  191.9 0.6 collective-permute-start.5
  192.5 112.8 %add_bitcast_fusion.1 = f32[1,512,2048]{2,1,0:T(8,128)} fusion(s32[512,2048]{1,0:T(8,128)S(1)} %copy-done.8, f32[]{:T(128)} %bitcast.96, f32[]{:T(128)} %bitcast.95, f32[]{:T(128)} %bitcast.94, f32[]{:T(128)} %bitcast.93, f32[]{:T(128)} %bitcast.92, f32[]{:T(128)} %bitcast.91, f32[]{:T(128)} %bitcast.90, f32[]{:T(128)} %bitcast.89, f32[]{:T(128)} %bitcast.88, ...), kind=kLoop, calls=%fused_computation.12 | loop fusion | flops 269484032 | bytes 8388992 | tf_op jit(solution)/shard_map/while/body/eval_jaxpr/stack | solution.py:37
  305.3 1.3 fusion.3
  306.7 8.5 %select_maximum_fusion = f32[2,512,2561]{2,1,0:T(8,128)} fusion(f32[1,512,2048]{2,1,0:T(8,128)} %add_bitcast_fusion, f32[1,512,2048]{2,1,0:T(8,128)} %add_bitcast_fusion.1), kind=kLoop, calls=%fused_computation | loop fusion | flops 10489856 | bytes 18878464 | tf_op jit(solution)/shard_map/while/body/eval_jaxpr/stack | solution.py:37
  315.2 15.9 %reshape.119 = f32[2622464]{0:T(1024)} reshape(f32[2,512,2561]{2,1,0:T(8,128)} %select_maximum_fusion) | data formatting | bytes 20979712
  331.1 16.6 %reshape.115 = f32[2,1311232]{1,0:T(2,128)} reshape(f32[2622464]{0:T(1024)} %reshape.119) | data formatting | bytes 20979712 | tf_op jit(solution)/shard_map/while/body/eval_jaxpr/reshape | solution.py:21
  347.7 8.4 %slice.977 = f32[2,1310720]{1,0:T(2,128)} slice(f32[2,1311232]{1,0:T(2,128)} %reshape.115), slice={[0:2], [0:1310720]} | slice | bytes 20971520 | tf_op jit(solution)/shard_map/while/body/eval_jaxpr/slice | solution.py:22
  356.2 0.0 all-to-all-done
  356.2 0.1 reshape_reshape.4
  356.3 0.0 collective-permute-done.5
  356.3 2.0 broadcast_select_fusion.1
  358.3 1.4 slice_bitcast_fusion
  359.7 1.6 copy.14
  361.3 10.8 %fusion.23 = (f32[2,512]{1,0:T(2,128)S(1)}, f32[2,512,2560]{2,1,0:T(8,128)}) fusion(f32[1,2,512,2560]{3,1,2,0:T(2,128)} %bitcast.224, bf16[320,2,8,128]{3,2,1,0:T(8,128)(2,1)} %get-tuple-element.31, bf16[512,2,128]{2,1,0:T(2,128)(2,1)S(1)} %reshape_reshape.4, pred[512,2560]{1,0:T(8,128)(4,1)S(1)} %fusion.3), kind=kOutput, calls=%fused_computation.48 | convolution fusion | flops 681573376 | bytes 23859200 | tf_op jit(solution)/shard_map/while/body/eval_jaxpr/ihd,khd->hik/dot_general | solution.py:89
  372.1 19.1 %pmax.7 = f32[2,512]{1,0:T(2,128)S(1)} all-reduce(f32[2,512]{1,0:T(2,128)S(1)} %get-tuple-element.250), channel_id=1, replica_groups=mesh['pb'=16,'ka'=8] {'ka'}, use_global_device_ids=true, to_apply=%region_1.2 | all-reduce | flops 1024 | bytes 8192 | tf_op jit(solution)/shard_map/pmax | solution.py:104
  391.1 6.7 %fusion.4 = f32[2,128,512]{2,1,0:T(8,128)} fusion(bf16[2560,2,128]{0,2,1:T(8,128)(2,1)S(1)} %bitcast.225, f32[2,512,2560]{2,1,0:T(8,128)} %get-tuple-element.251, f32[2,512]{1,0:T(2,128)S(1)} %pmax.7), kind=kOutput, calls=%fused_computation.17 | convolution fusion | flops 676331520 | bytes 12324864 | tf_op jit(solution)/shard_map/while/body/eval_jaxpr/hik,khd->ihd/dot_general | solution.py:112
  397.9 0.0 all-reduce.3.cloned.1.call-update
  397.9 0.0 copy-start.6
  397.9 0.0 copy-start.1
  397.9 5.6 %convert_reduce_fusion = f32[2,512]{1,0:T(2,128)S(1)} fusion(f32[2,512,2560]{2,1,0:T(8,128)} %get-tuple-element.251, f32[2,512]{1,0:T(2,128)S(1)} %pmax.7), kind=kLoop, calls=%fused_computation.4 | loop fusion | flops 10484736 | bytes 10493952 | tf_op jit(solution)/shard_map/while/body/eval_jaxpr/reduce_sum | solution.py:109
  403.6 16.0 %psum.15 = f32[512,2]{0,1:T(2,128)S(1)} all-reduce(f32[512,2]{0,1:T(2,128)S(1)} %bitcast.227), channel_id=1, replica_groups=mesh['pb'=16,'ka'=8] {'ka'}, use_global_device_ids=true, to_apply=%region_4.5 | all-reduce | flops 1024 | bytes 8192 | tf_op jit(solution)/shard_map/psum | solution.py:121
  419.6 0.1 constant_dynamic-slice_fusion
  419.7 68.0 %all-reduce.3.cloned.1.call-done = f32[512,256]{0,1:T(8,128)} async-done(((f32[512,256]{0,1:T(8,128)}), f32[512,256]{0,1:T(8,128)}) %all-reduce.3.cloned.1.call-update) | async-done | bytes 524304 | tf_op jit(solution)/shard_map/psum | solution.py:121
  487.7 1.0 fusion.8
  488.7 0.0 copy-done.6
  488.7 1.0 convolution_convert_fusion
  (14 shorter events, 0.0 us)
Async XLA Ops:
  6.5 1.4 copy-start
  6.5 46.9 %copy-start.3 = (f32[2,32]{1,0:T(2,128)S(1)}, f32[2,32]{1,0:T(2,128)}, u32[]{:S(2)}) copy-start(f32[2,32]{1,0:T(2,128)} %param.13) | copy-start | bytes 772
  6.5 48.4 %copy-start.4 = (f32[2,32]{1,0:T(2,128)S(1)}, f32[2,32]{1,0:T(2,128)}, u32[]{:S(2)}) copy-start(f32[2,32]{1,0:T(2,128)} %param.12) | copy-start | bytes 772
  6.5 49.9 %copy-start.5 = (f32[2,32]{1,0:T(2,128)S(1)}, f32[2,32]{1,0:T(2,128)}, u32[]{:S(2)}) copy-start(f32[2,32]{1,0:T(2,128)} %param.14) | copy-start | bytes 772
  40.7 20.1 %collective-permute-start = (bf16[512,512]{1,0:T(8,128)(2,1)S(1)}, bf16[512,512]{1,0:T(8,128)(2,1)S(1)}, u32[]{:S(2)}, u32[]{:S(2)}) collective-permute-start(bf16[512,512]{1,0:T(8,128)(2,1)S(1)} %all_gather.3), channel_id=1, source_target_pairs={{8,0},{16,8},{24,16},{32,24},{40,32},{48,40},{56,48},{64,56},{72,6... | collective-permute-start | bytes 1572872 | tf_op jit(solution)/shard_map/ppermute | solution.py:15
  40.7 26.8 %collective-permute-start.1 = (bf16[512,512]{1,0:T(8,128)(2,1)S(1)}, bf16[512,512]{1,0:T(8,128)(2,1)S(1)}, u32[]{:S(2)}, u32[]{:S(2)}) collective-permute-start(bf16[512,512]{1,0:T(8,128)(2,1)S(1)} %all_gather.3), channel_id=1, source_target_pairs={{16,0},{24,8},{32,16},{40,24},{48,32},{56,40},{64,48},{72,56},{80,... | collective-permute-start | bytes 1572872 | tf_op jit(solution)/shard_map/ppermute | solution.py:15
  46.1 22.2 %collective-permute-start.2 = (bf16[512,512]{1,0:T(8,128)(2,1)S(1)}, bf16[512,512]{1,0:T(8,128)(2,1)S(1)}, u32[]{:S(2)}, u32[]{:S(2)}) collective-permute-start(bf16[512,512]{1,0:T(8,128)(2,1)S(1)} %all_gather.3), channel_id=1, source_target_pairs={{24,0},{32,8},{40,16},{48,24},{56,32},{64,40},{72,48},{80,56},{88,... | collective-permute-start | bytes 1572872 | tf_op jit(solution)/shard_map/ppermute | solution.py:15
  46.7 22.5 %collective-permute-start.3 = (bf16[512,512]{1,0:T(8,128)(2,1)S(1)}, bf16[512,512]{1,0:T(8,128)(2,1)S(1)}, u32[]{:S(2)}, u32[]{:S(2)}) collective-permute-start(bf16[512,512]{1,0:T(8,128)(2,1)S(1)} %all_gather.3), channel_id=1, source_target_pairs={{32,0},{40,8},{48,16},{56,24},{64,32},{72,40},{80,48},{88,56},{96,... | collective-permute-start | bytes 1572872 | tf_op jit(solution)/shard_map/ppermute | solution.py:15
  49.3 306.9 %all-to-all-start = ((bf16[8,64,256]{2,1,0:T(8,128)(2,1)}), bf16[8,64,256]{2,1,0:T(8,128)(2,1)S(1)}, u32[]{:S(2)}, u32[]{:S(2)}) async-start(bf16[8,64,256]{2,1,0:T(8,128)(2,1)} %stack.11), calls=%async_computation | async-start | bytes 524288 | tf_op jit(solution)/shard_map/all_to_all | solution.py:48
  53.4 434.3 %all-reduce.3.cloned.1.call-start = ((), (), s32[]{:S(2)}) async-start(), calls=%async_computation.1 | async-start | bytes 1048576 | tf_op jit(solution)/shard_map/psum | solution.py:121
  53.5 19.5 %copy-start.7 = (s32[512,2048]{1,0:T(8,128)S(1)}, s32[512,2048]{1,0:T(8,128)}, u32[]{:S(2)}) copy-start(s32[512,2048]{1,0:T(8,128)} %param.9) | copy-start | bytes 12582916
  70.0 118.3 %collective-permute-start.4 = (bf16[2560,512]{1,0:T(8,128)(2,1)}, bf16[2560,512]{1,0:T(8,128)(2,1)}, u32[]{:S(2)}, u32[]{:S(2)}) collective-permute-start(bf16[2560,512]{1,0:T(8,128)(2,1)} %constant_dynamic-update-slice_fusion), channel_id=1, source_target_pairs={{32,0},{40,8},{48,16},{56,24},{64,32},{72,40},{80,48},{88,56},{96,... | collective-permute-start | bytes 7864328 | tf_op jit(solution)/shard_map/ppermute | solution.py:15
  186.1 6.4 %copy-start.8 = (s32[512,2048]{1,0:T(8,128)S(1)}, s32[512,2048]{1,0:T(8,128)}, u32[]{:S(2)}) copy-start(s32[512,2048]{1,0:T(8,128)} %param.9) | copy-start | bytes 12582916
  191.9 164.4 %collective-permute-start.5 = (bf16[2560,512]{1,0:T(8,128)(2,1)}, bf16[2560,512]{1,0:T(8,128)(2,1)}, u32[]{:S(2)}, u32[]{:S(2)}) collective-permute-start(bf16[2560,512]{1,0:T(8,128)(2,1)} %broadcast_select_fusion), channel_id=1, source_target_pairs={{64,0},{72,8},{80,16},{88,24},{96,32},{104,40},{112,48},{120,56},{... | collective-permute-start | bytes 7864328 | tf_op jit(solution)/shard_map/ppermute | solution.py:15
  361.3 29.9 %copy-start.2 = (bf16[2560,256]{0,1:T(8,128)(2,1)S(1)}, bf16[2560,256]{0,1:T(8,128)(2,1)}, u32[]{:S(2)}) copy-start(bf16[2560,256]{0,1:T(8,128)(2,1)} %copy.14) | copy-start | bytes 3932164
  397.9 90.8 %copy-start.6 = (bf16[256,1536]{1,0:T(8,128)(2,1)S(1)}, bf16[256,1536]{1,0:T(8,128)(2,1)}, u32[]{:S(2)}) copy-start(bf16[256,1536]{1,0:T(8,128)(2,1)} %param.15) | copy-start | bytes 2359300
  397.9 91.8 %copy-start.1 = (bf16[1536,512]{1,0:T(8,128)(2,1)S(1)}, bf16[1536,512]{1,0:T(8,128)(2,1)}, u32[]{:S(2)}) copy-start(bf16[1536,512]{1,0:T(8,128)(2,1)} %param.11) | copy-start | bytes 4718596
Sparse Core Ops, SparseCore 0:
  398.0 89.6 all-reduce.2
